TPU v7x, 256 devices: a whole 4x4x8 slice. The times are simulated.
256 devices in a mesh: loop: 16 (over x, z_lo), rep: 16 (over z_hi, y, core).
Axes of the slice: x: 4, y: 4, z: 8 (z_hi: 2, z_lo: 4; z = z_hi * 4 + z_lo), core: 2. Of those that a mesh axis runs over, the one named last changes fastest.
Arguments:
- features: float32 [8192, 128], P('loop'), may hold values from -6 to 6
- weight: float32 [128, 256], replicated, may hold values from -0.5 to 0.5
- bias: float32 [256], replicated, may hold values from -3 to 3
- tile_values: float32 [4096, 128, 128], P(('loop', 'rep')), may hold values from -0.125 to 0.125
- tile_rows: int32 [4096], P(('loop', 'rep')), may hold values from 0 to 63, as said below
- tile_cols: int32 [4096], P(('loop', 'rep')), may hold values from 0 to 63, as said below
- tile_count: int32 [256], P(('loop', 'rep')), may hold values from 1 to 16, as said below
- cotangent: float32 [8192, 256], P('loop'), may hold values from -0.6 to 0.6
Outputs:
- output: float32 [8192, 256], P('loop')
- grad_features: float32 [8192, 128], P('loop')
- grad_weight: float32 [128, 256], replicated
- grad_bias: float32 [256], replicated
Inputs may be any that keep to these rules, and one draw needn't show every extreme that they name: `tile_rows`: every slot of a device at loop index l names a row block from l * 4 to (l + 1) * 4 - 1. `tile_cols`: for every loop index m, the live slots of one device name at most 2 different column blocks from m * 4 to (m + 1) * 4 - 1; for every loop index some device names exactly 2 of one such range. `tile_count`: for every loop index some device has all 16 slots live.
All inputs are finite; a program needn't handle non-finite values.
Results may differ from a plain program's by a relative error of at most 0.0001.
Values sent between devices are 32-bit elements; how exact they have to be, the bound alone decides.
A program may use at most 64 MiB of HBM per device.

v0:
```python
import jax
import jax.numpy as jnp
from jax import lax
from jax.sharding import PartitionSpec as P


def per_device(features, weight, bias, tile_values, tile_rows, tile_cols, tile_count, cotangent):
    highest = lax.Precision.HIGHEST
    tile_side = tile_values.shape[1]
    rows_here = features.shape[0]
    nblocks = rows_here // tile_side
    slots = tile_values.shape[0]
    local_rows = tile_rows - lax.axis_index("loop") * nblocks
    live_slot = (jnp.arange(slots, dtype=jnp.int32) < tile_count[0]).astype(jnp.float32)
    row_pick = (local_rows[:, None] == jnp.arange(nblocks, dtype=jnp.int32)[None, :]).astype(
        jnp.float32
    )
    row_pick = row_pick * live_slot[:, None]
    moved = jnp.dot(features, weight, precision=highest)
    gathered = lax.all_gather(moved, "loop", axis=0, tiled=True)
    width = gathered.shape[1]
    blocks = gathered.reshape(-1, tile_side, width)[tile_cols]
    products = jnp.einsum("kij,kjf->kif", tile_values, blocks, precision=highest)
    summed = lax.psum(
        jnp.einsum("kb,kif->bif", row_pick, products, precision=highest), "rep"
    ).reshape(rows_here, -1)
    preactive = summed + bias
    logistic = jax.nn.sigmoid(preactive)
    output = preactive * logistic
    gradient = cotangent * logistic * (1.0 + preactive * (1.0 - logistic))
    source_blocks = gradient.reshape(nblocks, tile_side, gradient.shape[1])[
        jnp.clip(local_rows, 0, nblocks - 1)
    ]
    outgoing = jnp.einsum("kji,kjf->kif", tile_values, source_blocks, precision=highest)
    outgoing = outgoing * live_slot[:, None, None]
    span = rows_here * lax.axis_size("loop") // tile_side + 2
    column_pick = (tile_cols[:, None] == jnp.arange(span, dtype=jnp.int32)[None, :]).astype(
        jnp.float32
    )
    placed = jnp.einsum("kb,kif->bif", column_pick, outgoing, precision=highest)
    placed = placed.reshape(span * tile_side, outgoing.shape[2])
    term = lax.psum_scatter(
        lax.slice_in_dim(placed, 0, rows_here * lax.axis_size("loop"), axis=0),
        "loop",
        scatter_dimension=0,
        tiled=True,
    )
    own_rows = lax.psum(term, "rep")
    weight_term = jnp.dot(features.T, own_rows, precision=highest)
    grad_rows = jnp.dot(own_rows, weight.T, precision=highest)
    bias_term = jnp.sum(gradient, axis=0)
    grad_weight, grad_bias = lax.psum((weight_term, bias_term), "loop")
    return (output, grad_rows, grad_weight, grad_bias)


def solution(mesh):
    return jax.shard_map(
        per_device,
        mesh=mesh,
        in_specs=(
            P("loop", None),
            P(),
            P(),
            P(("loop", "rep"), None, None),
            P(("loop", "rep")),
            P(("loop", "rep")),
            P(("loop", "rep")),
            P("loop", None),
        ),
        out_specs=(P("loop", None), P("loop", None), P(), P()),
        check_vma=False,
    )
```

profile of v0, /device:TPU:8, one launch (start us, length us, event | category | flops | bytes accessed | tf_op | source)
XLA Modules:
  0.0 953.2 jit_solution(14281771124516442620)
XLA Ops:
  7.2 0.0 all-gather.2.cloned.1.call-start
  7.2 2.4 fusion.16
  9.7 0.0 all-gather.2.cloned.1.call-update
  9.7 0.0 all-reduce.4.cloned.1.call-start
  10.4 0.7 compare_select_fusion.1
  11.1 0.7 compare_select_fusion
  11.7 189.3 %all-gather.2.cloned.1.call-done = f32[8192,256]{1,0:T(8,128)} async-done(((f32[512,256]{1,0:T(8,128)}), f32[8192,256]{1,0:T(8,128)}) %all-gather.2.cloned.1.call-update) | async-done | bytes 8388624 | tf_op jit(solution)/shard_map/all_gather | solution.py:20
  201.0 4.1 gather_fusion
  205.1 5.1 fusion.17
  210.2 2.2 copy.16
  212.5 1.1 fusion.2
  213.6 0.9 copy.13
  214.5 0.0 all-reduce.4.cloned.1.call-update
  214.5 0.0 reduce-scatter.2.cloned.1.call-start
  214.6 0.1 fusion.7
  214.7 168.0 %all-reduce.4.cloned.1.call-done = f32[512,256]{1,0:T(8,128)} async-done(((f32[512,256]{1,0:T(8,128)}), f32[512,256]{1,0:T(8,128)}) %all-reduce.4.cloned.1.call-update) | async-done | bytes 524304 | tf_op jit(solution)/shard_map/psum | solution.py:24
  382.6 2.2 fusion.15
  384.9 2.0 gather_fusion.1
  386.9 5.3 fusion.18
  392.2 2.2 copy.17
  394.4 5.2 fusion
  399.6 8.1 copy.14
  407.7 0.0 reduce-scatter.2.cloned.1.call-update
  407.7 0.0 all-reduce.6.cloned.1.call-start
  407.8 196.3 %reduce-scatter.2.cloned.1.call-done = f32[512,256]{1,0:T(8,128)} async-done(((f32[8192,256]{1,0:T(8,128)}), f32[512,256]{1,0:T(8,128)}) %reduce-scatter.2.cloned.1.call-update) | async-done | bytes 524304 | tf_op jit(solution)/shard_map/reduce_scatter | solution.py:42
  604.1 0.0 all-reduce.8.cloned.1.call-start
  604.1 40.0 %psum.31 = f32[256]{0:T(256)} all-reduce(f32[256]{0:T(256)S(1)} %get-tuple-element.12), channel_id=1, replica_groups=mesh['loop'=16,'rep'=16] {'loop'}, use_global_device_ids=true, to_apply=%region_5.6 | all-reduce | flops 256 | bytes 2048 | tf_op jit(solution)/shard_map/psum | solution.py:52
  644.1 130.8 %all-reduce.6.cloned.1.call-done = f32[512,256]{1,0:T(8,128)} async-done(((f32[512,256]{1,0:T(8,128)}), f32[512,256]{1,0:T(8,128)}) %all-reduce.6.cloned.1.call-update) | async-done | bytes 524304 | tf_op jit(solution)/shard_map/psum | solution.py:48
  774.9 2.7 convolution_bitcast_fusion
  777.6 2.3 fusion.19
  780.0 165.1 %all-reduce.8.cloned.1.call-done = f32[128,256]{0,1:T(8,128)} async-done(((f32[128,256]{0,1:T(8,128)}), f32[128,256]{0,1:T(8,128)}) %all-reduce.8.cloned.1.call-update) | async-done | bytes 131088 | tf_op jit(solution)/shard_map/psum | solution.py:52
  945.0 1.7 copy.15
  (15 shorter events, 0.1 us)
Async XLA Ops:
  7.2 198.0 %copy-start = (f32[16,128,128]{2,1,0:T(8,128)S(1)}, f32[16,128,128]{2,1,0:T(8,128)}, u32[]{:S(2)}) copy-start(f32[16,128,128]{2,1,0:T(8,128)} %param.11) | copy-start | bytes 3145732
  7.2 193.9 %all-gather.2.cloned.1.call-start = ((), (), s32[]{:S(2)}) async-start(), calls=%async_computation.1 | async-start | bytes 8912896 | tf_op jit(solution)/shard_map/all_gather | solution.py:20
  9.7 373.0 %all-reduce.4.cloned.1.call-start = ((), (), s32[]{:S(2)}) async-start(), calls=%async_computation.2 | async-start | bytes 1048576 | tf_op jit(solution)/shard_map/psum | solution.py:24
  212.4 2.1 copy-start.4
  212.5 170.2 %copy-start.3 = (f32[256]{0:T(256)S(1)}, f32[256]{0:T(256)}, u32[]{:S(2)}) copy-start(f32[256]{0:T(256)} %param.10) | copy-start | bytes 3076
  214.5 389.5 %reduce-scatter.2.cloned.1.call-start = ((), (), s32[]{:S(2)}) async-start(), calls=%async_computation.3 | async-start | bytes 8912896 | tf_op jit(solution)/shard_map/reduce_scatter | solution.py:42
  407.7 367.2 %copy-start.1 = (f32[512,128]{1,0:T(8,128)S(1)}, f32[512,128]{1,0:T(8,128)}, u32[]{:S(2)}) copy-start(f32[512,128]{1,0:T(8,128)} %param.8) | copy-start | bytes 786436
  407.7 369.9 %copy-start.2 = (f32[128,256]{1,0:T(8,128)S(1)}, f32[128,256]{1,0:T(8,128)}, u32[]{:S(2)}) copy-start(f32[128,256]{1,0:T(8,128)} %param.9) | copy-start | bytes 393220
  407.7 367.2 %all-reduce.6.cloned.1.call-start = ((), (), s32[]{:S(2)}) async-start(), calls=%async_computation.4 | async-start | bytes 1048576 | tf_op jit(solution)/shard_map/psum | solution.py:48
  604.1 341.0 %all-reduce.8.cloned.1.call-start = ((), (), s32[]{:S(2)}) async-start(), calls=%async_computation.5 | async-start | bytes 262144 | tf_op jit(solution)/shard_map/psum | solution.py:52
Sparse Core Ops, SparseCore 0:
  10.4 190.6 all-gather.1
  214.6 167.9 all-reduce.3
  407.8 196.1 reduce-scatter.1
  606.7 168.1 all-reduce.5
  777.9 167.0 all-reduce.7
where the time goes:
time: 954 us; the launch traced here: 953 us
  waiting for transfers between devices  850 us (89%)
  blocking collectives  40 us (4%)
  matrix products  24.1 us (3%)
  local copies, waits for them, and re-layouts  21.2 us (2%)
  between operations  14.5 us (2%)
    reduce_scatter x1, waiting for transfers between devices, per_device(): lax.psum_scatter(lax.slice_in_dim(placed, 0, rows_here * lax.axis_size('l...  196 us
    all_gather x1, waiting for transfers between devices, per_device(): gathered = lax.all_gather(moved, 'loop', axis=0, tiled=True)  189 us
    psum x1, waiting for transfers between devices, per_device(): lax.psum(jnp.einsum('kb,kif->bif', row_pick, products, precision=highest)...  168 us
    psum x1, waiting for transfers between devices, per_device(): grad_weight, grad_bias = lax.psum((weight_term, bias_term), 'loop')  165 us
    psum x1, waiting for transfers between devices, per_device(): own_rows = lax.psum(term, 'rep')  131 us
    psum x1, blocking collectives, per_device(): grad_weight, grad_bias = lax.psum((weight_term, bias_term), 'loop')  40 us
  transfers between devices with their start and end apart: 5, of which 5 were waited for; matrix products, arithmetic and copies ran while one was open for 0% of the time, Pallas kernels for 0%

commit v1 on v0

--- a/solution.py
+++ b/solution.py
@@ -2,6 +2,13 @@
 import jax.numpy as jnp
 from jax import lax
 from jax.sharding import PartitionSpec as P
+
+
+def swapped_in(array, axis, d):
+    peers = lax.axis_size(axis)
+    blocks = jnp.stack([array for _ in range(peers)])
+    blocks = lax.all_to_all(blocks, axis, split_axis=0, concat_axis=0)
+    return jnp.concatenate(blocks, axis=d)
 
 
 def per_device(features, weight, bias, tile_values, tile_rows, tile_cols, tile_count, cotangent):
@@ -17,7 +24,7 @@
     )
     row_pick = row_pick * live_slot[:, None]
     moved = jnp.dot(features, weight, precision=highest)
-    gathered = lax.all_gather(moved, "loop", axis=0, tiled=True)
+    gathered = swapped_in(moved, "loop", 0)
     width = gathered.shape[1]
     blocks = gathered.reshape(-1, tile_side, width)[tile_cols]
     products = jnp.einsum("kij,kjf->kif", tile_values, blocks, precision=highest)

time: 954 us -> 961 us (level)
    all_gather x1 -> x0, waiting for transfers between devices: 189 us -> none  [per_device(): gathered = lax.all_gather(moved, 'loop', axis=0, tiled=True)]
    all_to_all x0 -> x1, waiting for transfers between devices: none -> 185 us  [swapped_in(): blocks = lax.all_to_all(blocks, axis, split_axis=0, concat_axis=0)]
where the time goes in v1:
time: 961 us
  waiting for transfers between devices  847 us (88%)
  blocking collectives  40 us (4%)
  local copies, waits for them, and re-layouts  25.2 us (3%)
  matrix products  23.4 us (2%)
  between operations  14.6 us (2%)
    reduce_scatter x1, waiting for transfers between devices, per_device(): lax.psum_scatter(lax.slice_in_dim(placed, 0, rows_here * lax.axis_size('l...  196 us
    all_to_all x1, waiting for transfers between devices, swapped_in(): blocks = lax.all_to_all(blocks, axis, split_axis=0, concat_axis=0)  185 us
    psum x1, waiting for transfers between devices, per_device(): lax.psum(jnp.einsum('kb,kif->bif', row_pick, products, precision=highest)...  169 us
    psum x1, waiting for transfers between devices, per_device(): grad_weight, grad_bias = lax.psum((weight_term, bias_term), 'loop')  165 us
    psum x1, waiting for transfers between devices, per_device(): own_rows = lax.psum(term, 'rep')  131 us
    psum x1, blocking collectives, per_device(): grad_weight, grad_bias = lax.psum((weight_term, bias_term), 'loop')  40 us
  transfers between devices with their start and end apart: 5, of which 5 were waited for; matrix products, arithmetic and copies ran while one was open for 0% of the time, Pallas kernels for 0%

profile of v1, /device:TPU:8, one launch (start us, length us, event | category | flops | bytes accessed | tf_op | source)
XLA Modules:
  0.0 960.8 jit_solution(1751617026336383926)
XLA Ops:
  7.2 1.6 fusion.16
  8.8 4.0 stack.2
  12.9 8.7 all-to-all-start
  21.5 0.0 all-reduce.4.cloned.1.call-start
  22.3 185.3 %all-to-all-done = f32[16,512,256]{2,1,0:T(8,128)} async-done(((f32[16,512,256]{2,1,0:T(8,128)}), f32[16,512,256]{2,1,0:T(8,128)}, u32[]{:S(2)}, u32[]{:S(2)}) %all-to-all-start) | async-done | bytes 8388640 | tf_op jit(solution)/shard_map/all_to_all | solution.py:10
  207.6 4.1 gather_fusion
  211.7 5.1 fusion.17
  216.8 2.2 copy.16
  219.0 1.1 fusion.2
  220.2 0.9 copy.13
  221.0 0.0 all-reduce.4.cloned.1.call-update
  221.1 0.0 reduce-scatter.2.cloned.1.call-start
  221.1 0.1 fusion.7
  221.2 168.9 %all-reduce.4.cloned.1.call-done = f32[512,256]{1,0:T(8,128)} async-done(((f32[512,256]{1,0:T(8,128)}), f32[512,256]{1,0:T(8,128)}) %all-reduce.4.cloned.1.call-update) | async-done | bytes 524304 | tf_op jit(solution)/shard_map/psum | solution.py:31
  390.1 2.2 fusion.15
  392.3 2.0 gather_fusion.1
  394.3 5.3 fusion.18
  399.6 2.2 copy.17
  401.9 5.2 fusion
  407.1 8.1 copy.14
  415.1 0.0 reduce-scatter.2.cloned.1.call-update
  415.2 0.0 all-reduce.6.cloned.1.call-start
  415.2 196.3 %reduce-scatter.2.cloned.1.call-done = f32[512,256]{1,0:T(8,128)} async-done(((f32[8192,256]{1,0:T(8,128)}), f32[512,256]{1,0:T(8,128)}) %reduce-scatter.2.cloned.1.call-update) | async-done | bytes 524304 | tf_op jit(solution)/shard_map/reduce_scatter | solution.py:49
  611.5 0.0 all-reduce.6.cloned.1.call-update
  611.5 0.0 all-reduce.8.cloned.1.call-start
  611.6 40.0 %psum.31 = f32[256]{0:T(256)} all-reduce(f32[256]{0:T(256)S(1)} %get-tuple-element.12), channel_id=1, replica_groups=mesh['loop'=16,'rep'=16] {'loop'}, use_global_device_ids=true, to_apply=%region_5.6 | all-reduce | flops 256 | bytes 2048 | tf_op jit(solution)/shard_map/psum | solution.py:59
  651.5 131.0 %all-reduce.6.cloned.1.call-done = f32[512,256]{1,0:T(8,128)} async-done(((f32[512,256]{1,0:T(8,128)}), f32[512,256]{1,0:T(8,128)}) %all-reduce.6.cloned.1.call-update) | async-done | bytes 524304 | tf_op jit(solution)/shard_map/psum | solution.py:55
  782.5 2.7 convolution_bitcast_fusion
  785.2 0.0 all-reduce.8.cloned.1.call-update
  785.2 2.3 fusion.19
  787.5 165.1 %all-reduce.8.cloned.1.call-done = f32[128,256]{0,1:T(8,128)} async-done(((f32[128,256]{0,1:T(8,128)}), f32[128,256]{0,1:T(8,128)}) %all-reduce.8.cloned.1.call-update) | async-done | bytes 131088 | tf_op jit(solution)/shard_map/psum | solution.py:59
  952.6 1.7 copy.15
  (17 shorter events, 0.1 us)
Async XLA Ops:
  7.2 204.5 %copy-start = (f32[16,128,128]{2,1,0:T(8,128)S(1)}, f32[16,128,128]{2,1,0:T(8,128)}, u32[]{:S(2)}) copy-start(f32[16,128,128]{2,1,0:T(8,128)} %param.11) | copy-start | bytes 3145732
  12.9 9.4 copy-start.4
  12.9 9.4 copy-start.5
  12.9 194.8 %all-to-all-start = ((f32[16,512,256]{2,1,0:T(8,128)}), f32[16,512,256]{2,1,0:T(8,128)}, u32[]{:S(2)}, u32[]{:S(2)}) async-start(f32[16,512,256]{2,1,0:T(8,128)} %stack.2), calls=%async_computation | async-start | bytes 16777216 | tf_op jit(solution)/shard_map/all_to_all | solution.py:10
  21.5 368.6 %all-reduce.4.cloned.1.call-start = ((), (), s32[]{:S(2)}) async-start(), calls=%async_computation.2 | async-start | bytes 1048576 | tf_op jit(solution)/shard_map/psum | solution.py:31
  219.0 171.1 %copy-start.3 = (f32[256]{0:T(256)S(1)}, f32[256]{0:T(256)}, u32[]{:S(2)}) copy-start(f32[256]{0:T(256)} %param.10) | copy-start | bytes 3076
  221.1 390.4 %reduce-scatter.2.cloned.1.call-start = ((), (), s32[]{:S(2)}) async-start(), calls=%async_computation.3 | async-start | bytes 8912896 | tf_op jit(solution)/shard_map/reduce_scatter | solution.py:49
  415.1 367.4 %copy-start.1 = (f32[512,128]{1,0:T(8,128)S(1)}, f32[512,128]{1,0:T(8,128)}, u32[]{:S(2)}) copy-start(f32[512,128]{1,0:T(8,128)} %param.8) | copy-start | bytes 786436
  415.1 370.1 %copy-start.2 = (f32[128,256]{1,0:T(8,128)S(1)}, f32[128,256]{1,0:T(8,128)}, u32[]{:S(2)}) copy-start(f32[128,256]{1,0:T(8,128)} %param.9) | copy-start | bytes 393220
  415.2 367.3 %all-reduce.6.cloned.1.call-start = ((), (), s32[]{:S(2)}) async-start(), calls=%async_computation.4 | async-start | bytes 1048576 | tf_op jit(solution)/shard_map/psum | solution.py:55
  611.5 341.1 %all-reduce.8.cloned.1.call-start = ((), (), s32[]{:S(2)}) async-start(), calls=%async_computation.5 | async-start | bytes 262144 | tf_op jit(solution)/shard_map/psum | solution.py:59
Sparse Core Ops, SparseCore 0:
  221.2 168.8 all-reduce.3
  415.3 196.1 reduce-scatter.1
  614.3 168.1 all-reduce.5
  785.5 167.0 all-reduce.7

commit v2 on v0

--- a/solution.py
+++ b/solution.py
@@ -2,6 +2,8 @@
 import jax.numpy as jnp
 from jax import lax
 from jax.sharding import PartitionSpec as P
+
+_produce_core = lambda a0: lax.all_gather(a0, "rep").sum(axis=0)
 
 
 def per_device(features, weight, bias, tile_values, tile_rows, tile_cols, tile_count, cotangent):
@@ -45,7 +47,7 @@
         scatter_dimension=0,
         tiled=True,
     )
-    own_rows = lax.psum(term, "rep")
+    own_rows = _produce_core(term)
     weight_term = jnp.dot(features.T, own_rows, precision=highest)
     grad_rows = jnp.dot(own_rows, weight.T, precision=highest)
     bias_term = jnp.sum(gradient, axis=0)

time: 954 us -> 881 us (0.923)
  waiting for transfers between devices: 850 us -> 775 us
    psum x1 -> x0, waiting for transfers between devices: 131 us -> none  [per_device(): own_rows = lax.psum(term, 'rep')]
    all_gather x0 -> x1, waiting for transfers between devices: none -> 67.5 us  [_produce_core = lambda a0: lax.all_gather(a0, 'rep').sum(axis=0)]
    psum x1, waiting for transfers between devices: 165 us -> 153 us  [per_device(): grad_weight, grad_bias = lax.psum((weight_term, bias_term), 'loop')]
where the time goes in v2:
time: 881 us
  waiting for transfers between devices  775 us (88%)
  blocking collectives  40.7 us (5%)
  matrix products  22.1 us (3%)
  local copies, waits for them, and re-layouts  21.2 us (2%)
  between operations  14.5 us (2%)
    reduce_scatter x1, waiting for transfers between devices, per_device(): lax.psum_scatter(lax.slice_in_dim(placed, 0, rows_here * lax.axis_size('l...  196 us
    all_gather x1, waiting for transfers between devices, per_device(): gathered = lax.all_gather(moved, 'loop', axis=0, tiled=True)  189 us
    psum x1, waiting for transfers between devices, per_device(): lax.psum(jnp.einsum('kb,kif->bif', row_pick, products, precision=highest)...  168 us
    psum x1, waiting for transfers between devices, per_device(): grad_weight, grad_bias = lax.psum((weight_term, bias_term), 'loop')  153 us
    all_gather x1, waiting for transfers between devices, _produce_core = lambda a0: lax.all_gather(a0, 'rep').sum(axis=0)  67.5 us
    psum x1, blocking collectives, per_device(): grad_weight, grad_bias = lax.psum((weight_term, bias_term), 'loop')  40.7 us
  transfers between devices with their start and end apart: 5, of which 5 were waited for; matrix products, arithmetic and copies ran while one was open for 0% of the time, Pallas kernels for 0%

profile of v2, /device:TPU:8, one launch (start us, length us, event | category | flops | bytes accessed | tf_op | source)
XLA Modules:
  0.0 881.0 jit_solution(5528192498586917529)
XLA Ops:
  7.2 0.0 all-gather.4.cloned.1.call-start
  7.2 2.4 fusion.16
  9.7 0.0 all-gather.4.cloned.1.call-update
  9.7 0.0 all-reduce.3.cloned.1.call-start
  10.4 0.7 compare_select_fusion.1
  11.1 0.7 compare_select_fusion
  11.7 189.3 %all-gather.4.cloned.1.call-done = f32[8192,256]{1,0:T(8,128)} async-done(((f32[512,256]{1,0:T(8,128)}), f32[8192,256]{1,0:T(8,128)}) %all-gather.4.cloned.1.call-update) | async-done | bytes 8388624 | tf_op jit(solution)/shard_map/all_gather | solution.py:22
  201.0 4.1 gather_fusion
  205.1 5.1 fusion.17
  210.2 2.2 copy.16
  212.5 1.1 fusion.2
  213.6 0.9 copy.13
  214.5 0.0 all-reduce.3.cloned.1.call-update
  214.5 0.0 reduce-scatter.2.cloned.1.call-start
  214.6 0.1 fusion.7
  214.7 168.0 %all-reduce.3.cloned.1.call-done = f32[512,256]{1,0:T(8,128)} async-done(((f32[512,256]{1,0:T(8,128)}), f32[512,256]{1,0:T(8,128)}) %all-reduce.3.cloned.1.call-update) | async-done | bytes 524304 | tf_op jit(solution)/shard_map/psum | solution.py:26
  382.6 2.2 fusion.15
  384.9 2.0 gather_fusion.1
  386.9 5.3 fusion.18
  392.2 2.2 copy.17
  394.4 5.2 fusion
  399.6 8.1 copy.14
  407.7 0.0 all-gather.6.cloned.1.call-start
  407.8 196.3 %reduce-scatter.2.cloned.1.call-done = f32[512,256]{1,0:T(8,128)} async-done(((f32[8192,256]{1,0:T(8,128)}), f32[512,256]{1,0:T(8,128)}) %reduce-scatter.2.cloned.1.call-update) | async-done | bytes 524304 | tf_op jit(solution)/shard_map/reduce_scatter | solution.py:44
  604.1 0.0 all-reduce.5.cloned.1.call-start
  604.1 40.7 %psum.23 = f32[256]{0:T(256)} all-reduce(f32[256]{0:T(256)S(1)} %get-tuple-element.12), channel_id=1, replica_groups=mesh['loop'=16,'rep'=16] {'loop'}, use_global_device_ids=true, to_apply=%region_5.6 | all-reduce | flops 256 | bytes 2048 | tf_op jit(solution)/shard_map/psum | solution.py:54
  644.8 67.5 %all-gather.6.cloned.1.call-done = f32[8192,256]{1,0:T(8,128)} async-done(((f32[512,256]{1,0:T(8,128)}), f32[8192,256]{1,0:T(8,128)}) %all-gather.6.cloned.1.call-update) | async-done | bytes 8388624 | tf_op jit(solution)/shard_map/all_gather | solution.py:6
  712.3 4.0 reduce_sum.18
  716.4 1.7 convolution_bitcast_fusion
  718.1 1.3 fusion.19
  719.4 153.5 %all-reduce.5.cloned.1.call-done = f32[128,256]{0,1:T(8,128)} async-done(((f32[128,256]{0,1:T(8,128)}), f32[128,256]{0,1:T(8,128)}) %all-reduce.5.cloned.1.call-update) | async-done | bytes 131088 | tf_op jit(solution)/shard_map/psum | solution.py:54
  872.8 1.7 copy.15
  (16 shorter events, 0.1 us)
Async XLA Ops:
  7.2 198.0 %copy-start = (f32[16,128,128]{2,1,0:T(8,128)S(1)}, f32[16,128,128]{2,1,0:T(8,128)}, u32[]{:S(2)}) copy-start(f32[16,128,128]{2,1,0:T(8,128)} %param.11) | copy-start | bytes 3145732
  7.2 193.9 %all-gather.4.cloned.1.call-start = ((), (), s32[]{:S(2)}) async-start(), calls=%async_computation.1 | async-start | bytes 8912896 | tf_op jit(solution)/shard_map/all_gather | solution.py:22
  9.7 373.0 %all-reduce.3.cloned.1.call-start = ((), (), s32[]{:S(2)}) async-start(), calls=%async_computation.2 | async-start | bytes 1048576 | tf_op jit(solution)/shard_map/psum | solution.py:26
  212.4 2.1 copy-start.4
  212.5 170.2 %copy-start.3 = (f32[256]{0:T(256)S(1)}, f32[256]{0:T(256)}, u32[]{:S(2)}) copy-start(f32[256]{0:T(256)} %param.10) | copy-start | bytes 3076
  214.5 389.5 %reduce-scatter.2.cloned.1.call-start = ((), (), s32[]{:S(2)}) async-start(), calls=%async_computation.3 | async-start | bytes 8912896 | tf_op jit(solution)/shard_map/reduce_scatter | solution.py:44
  407.7 304.6 %all-gather.6.cloned.1.call-start = ((), (), s32[]{:S(2)}) async-start(), calls=%async_computation.5 | async-start | bytes 8912896 | tf_op jit(solution)/shard_map/all_gather | solution.py:6
  604.1 268.8 %all-reduce.5.cloned.1.call-start = ((), (), s32[]{:S(2)}) async-start(), calls=%async_computation.4 | async-start | bytes 262144 | tf_op jit(solution)/shard_map/psum | solution.py:54
  712.3 4.0 copy-start.1
  712.3 5.7 copy-start.2
Sparse Core Ops, SparseCore 0:
  10.4 190.6 all-gather.3
  214.6 167.9 all-reduce.2
  407.8 196.1 reduce-scatter.1
  607.0 105.3 all-gather.5
  718.2 154.6 all-reduce.4
